TPU v7x, 256 devices: a whole 4x4x8 slice. The times are simulated.
256 devices in a mesh: row: 32 (over z_hi, y, core), col: 8 (over z_lo, x).
Axes of the slice: x: 4, y: 4, z: 8 (z_hi: 4, z_lo: 2; z = z_hi * 2 + z_lo), core: 2. Of those that a mesh axis runs over, the one named last changes fastest.
Arguments:
- left: float32 [128, 16384], P('col', 'row'), may hold values from -12 to 12
- right: float32 [128, 16384], P('row', 'col'), may hold values from -12 to 12
- w_out: float32 [1024, 128], replicated, may hold values from -0.1875 to 0.1875
- b_out: float32 [128], replicated, may hold values from -3 to 3
- pair_grad: float32 [512, 512, 128], P('row', 'col'), may hold values from -6 to 6
Outputs:
- pair_out: float32 [512, 512, 128], P('row', 'col')
- grad_left: float32 [128, 16384], P('col', 'row')
- grad_right: float32 [128, 16384], P('row', 'col')
- grad_weight: float32 [1024, 128], replicated
- grad_bias: float32 [128], replicated
All inputs are finite; a program needn't handle non-finite values.
Results may differ from a plain program's by a relative error of at most 0.0001.
Values sent between devices are 32-bit elements; how exact they have to be, the bound alone decides.
No kernel may reach another device: no remote copies, remote signals or barrier semaphores. Data moves between devices by JAX's collectives and lax.ppermute only.
A program may use at most 128 MiB of HBM per device.

v0:
```python
import jax
import jax.numpy as jnp
from jax import lax
from jax.sharding import PartitionSpec as P

C = 32
Z = 128
S = 128


def body(left, right, w_out, b_out, pair_grad):
    highest = lax.Precision.HIGHEST
    tile_rows = left.shape[1] // C
    tile_cols = right.shape[1] // C
    residues = tile_rows * lax.axis_size("row")
    weight_cube = w_out.reshape(C, C, Z)
    contract_rows = (((0,), (0,)), ((), ()))
    contract_cols = (((1,), (1,)), ((), ()))
    left_all = lax.all_gather(left, "col", axis=0, tiled=True)
    right_all = lax.all_gather(right, "row", axis=0, tiled=True)
    outer = (
        lax.dot_general(
            left_all,
            right_all,
            contract_rows,
            precision=highest,
            preferred_element_type=jnp.float32,
        )
        / S
    )
    outer_split = outer.reshape(tile_rows, C, tile_cols, C)
    pair_out = jnp.einsum("icje,cez->ijz", outer_split, weight_cube, precision=highest) + b_out
    grad_outer = jnp.einsum("ijz,cez->icje", pair_grad, weight_cube, precision=highest)
    grad_outer = grad_outer.reshape(tile_rows * C, tile_cols * C)
    grad_left = lax.psum_scatter(
        lax.dot_general(
            right_all,
            grad_outer,
            contract_cols,
            precision=highest,
            preferred_element_type=jnp.float32,
        )
        / S,
        "col",
        scatter_dimension=0,
        tiled=True,
    )
    grad_right = lax.psum_scatter(
        jnp.dot(left_all, grad_outer, precision=highest) / S, "row", scatter_dimension=0, tiled=True
    )
    weight_term = jnp.einsum("icje,ijz->cez", outer_split, pair_grad, precision=highest).reshape(
        C * C, Z
    )
    bias_term = jnp.sum(pair_grad, axis=(0, 1))
    grad_weight, grad_bias = lax.psum((weight_term, bias_term), ("row", "col"))
    return (pair_out, grad_left, grad_right, grad_weight / residues, grad_bias / residues)


def solution(mesh):
    placed = (P("col", "row"), P("row", "col"), P(), P(), P("row", "col", None))
    return jax.shard_map(
        body,
        mesh=mesh,
        in_specs=placed,
        out_specs=(P("row", "col", None), P("col", "row"), P("row", "col"), P(), P()),
        check_vma=False,
    )
```

profile of v0, /device:TPU:8, one launch (start us, length us, event | category | flops | bytes accessed | tf_op | source)
XLA Modules:
  0.0 770.1 jit_solution(7213743941106208333)
XLA Ops:
  7.2 29.5 %all_gather.6 = f32[128,512]{1,0:T(8,128)S(1)} all-gather(f32[16,512]{1,0:T(8,128)} %param.5), channel_id=1, replica_groups=mesh['row'=32,'col'=8] {'col'}, dimensions={0}, use_global_device_ids=true | all-gather | bytes 294912 | tf_op jit(solution)/shard_map/all_gather | solution.py:19
  36.8 9.8 %convolution_bitcast_fusion = f32[16,32,64,32]{2,3,0,1:T(8,128)} fusion(f32[32,32,128,1]{2,1,3,0:T(8,128)S(1)} %bitcast.42, f32[16,64,128]{2,1,0:T(8,128)} %param.9), kind=kOutput, calls=%fused_computation.1 | convolution fusion | flops 1610612736 | bytes 5242880 | tf_op jit(solution)/shard_map/ijz,cez->icje/dot_general | solution.py:33
  46.6 12.3 %copy.21 = f32[16,32,64,32]{3,2,1,0:T(8,128)} copy(f32[16,32,64,32]{2,3,0,1:T(8,128)} %convolution_bitcast_fusion) | data formatting | bytes 8388608 | tf_op jit(solution)/shard_map/ijz,cez->icje/transpose | solution.py:33
  58.9 13.5 %reshape.24 = f32[512,2048]{1,0:T(8,128)} reshape(f32[16,32,64,32]{3,2,1,0:T(8,128)} %copy.21) | data formatting | bytes 8388608 | tf_op jit(solution)/shard_map/reshape | solution.py:34
  72.4 9.9 %fusion = f32[128,2048]{0,1:T(8,128)} fusion(f32[512,2048]{1,0:T(8,128)} %reshape.24, f32[128,512]{1,0:T(8,128)S(1)} %all_gather.6), kind=kOutput, calls=%fused_computation.3 | convolution fusion | flops 1610874880 | bytes 5505024 | tf_op jit(solution)/shard_map/dot_general | solution.py:49
  82.3 0.7 all-gather.3.cloned.1.call-update
  83.4 0.6 dynamic-slice
  84.7 77.5 %psum.15 = f32[128]{0:T(128)S(1)} all-reduce(f32[128]{0:T(128)S(1)} %reduce_sum.9), channel_id=1, replica_groups=mesh['row'=32,'col'=8] {'row','col'}, use_global_device_ids=true, to_apply=%region_4.0 | all-reduce | flops 128 | bytes 1024 | tf_op jit(solution)/shard_map/psum | solution.py:55
  162.1 0.5 broadcast_multiply_fusion.1
  162.6 205.9 %all-reduce.6.cloned.1.call-done = f32[128,2048]{0,1:T(8,128)} async-done(((f32[128,2048]{0,1:T(8,128)}), f32[128,2048]{0,1:T(8,128)}) %all-reduce.6.cloned.1.call-update) | async-done | bytes 1048592
  368.6 1.6 constant_dynamic-slice_fusion
  370.1 0.9 copy.25
  371.1 55.6 %all-gather.3.cloned.1.call-done = f32[32,4,2048]{2,1,0:T(4,128)} async-done(((f32[1,4,2048]{2,1,0:T(4,128)}), f32[32,4,2048]{2,1,0:T(4,128)}) %all-gather.3.cloned.1.call-update) | async-done | bytes 1048592 | tf_op jit(solution)/shard_map/all_gather | solution.py:20
  426.7 1.6 reshape.26
  428.3 5.0 convolution_multiply_fusion
  433.3 11.4 %reshape.22 = f32[16,32,64,32]{3,2,1,0:T(8,128)} reshape(f32[512,2048]{1,0:T(8,128)} %convolution_multiply_fusion) | data formatting | bytes 8388608 | tf_op jit(solution)/shard_map/reshape | solution.py:31
  444.7 12.7 %copy.33 = f32[32,32,16,64]{3,1,0,2:T(8,128)} copy(f32[32,32,16,64]{1,3,0,2:T(8,128)} %bitcast.44) | data formatting | bytes 8388608 | tf_op jit(solution)/shard_map/icje,ijz->cez/dot_general | solution.py:51
  457.4 9.9 %convolution_bitcast_fusion.2 = f32[1024,128]{1,0:T(8,128)} fusion(f32[1024,16,64]{2,0,1:T(8,128)} %bitcast.45, f32[16,64,128]{2,1,0:T(8,128)S(1)} %copy-done.1), kind=kOutput, calls=%fused_computation.5 | convolution fusion | flops 1610612736 | bytes 5242880 | tf_op jit(solution)/shard_map/icje,ijz->cez/dot_general | solution.py:51
  467.6 5.2 fusion.2
  472.8 0.8 copy.29
  473.7 17.6 %fusion.1 = f32[16,64,128]{2,1,0:T(8,128)} fusion(f32[16,32,64,32]{3,2,1,0:T(8,128)} %reshape.22, f32[32,32,128,1]{2,1,0,3:T(8,128)S(1)} %bitcast.43, f32[128]{0:T(128)S(1)} %copy-done.2), kind=kOutput, calls=%fused_computation.6 | convolution fusion | flops 1610743808 | bytes 5243392 | tf_op jit(solution)/shard_map/icje,cez->ijz/dot_general | solution.py:32
  491.3 230.2 %all-reduce.4.cloned.1.call-done = f32[1024,128]{1,0:T(8,128)} async-done(((f32[1024,128]{1,0:T(8,128)}), f32[1024,128]{1,0:T(8,128)}) %all-reduce.4.cloned.1.call-update) | async-done | bytes 524304 | tf_op jit(solution)/shard_map/psum | solution.py:55
  721.5 1.9 broadcast_multiply_fusion
  723.4 40.2 %reduce-scatter.5.cloned.1.call-done = f32[16,512]{1,0:T(8,128)} async-done(((f32[128,512]{1,0:T(8,128)}), f32[16,512]{1,0:T(8,128)}) %reduce-scatter.5.cloned.1.call-update) | async-done | bytes 32784
  (16 shorter events, 0.8 us)
Async XLA Ops:
  7.2 29.6 %copy-start = (f32[1024,128]{1,0:T(8,128)S(1)}, f32[1024,128]{1,0:T(8,128)}, u32[]{:S(2)}) copy-start(f32[1024,128]{1,0:T(8,128)} %param.7) | copy-start | bytes 1572868
  7.2 361.4 %all-reduce.6.cloned.1.call-start = ((), (), s32[]{:S(2)}) async-start(), calls=%async_computation.4 | async-start | bytes 2097152
  58.9 24.3 %copy-start.1 = (f32[16,64,128]{2,1,0:T(8,128)S(1)}, f32[16,64,128]{2,1,0:T(8,128)}, u32[]{:S(2)}) copy-start(f32[16,64,128]{2,1,0:T(8,128)} %param.9) | copy-start | bytes 1572868
  58.9 24.5 %copy-start.3 = (u32[256]{0:T(256)S(1)}, u32[256]{0:T(256)}, u32[]{:S(2)}) copy-start(u32[256]{0:T(256)} %constant.18) | copy-start | bytes 3076
  82.3 344.4 %all-gather.3.cloned.1.call-start = ((), (), s32[]{:S(2)}) async-start(), calls=%async_computation.2 | async-start | bytes 1081344 | tf_op jit(solution)/shard_map/all_gather | solution.py:20
  83.0 638.5 %all-reduce.4.cloned.1.call-start = ((), (), s32[]{:S(2)}) async-start(), calls=%async_computation.1 | async-start | bytes 1048576 | tf_op jit(solution)/shard_map/psum | solution.py:55
  457.4 16.3 %copy-start.2 = (f32[128]{0:T(128)S(1)}, f32[128]{0:T(128)}, u32[]{:S(2)}) copy-start(f32[128]{0:T(128)} %param.8) | copy-start | bytes 1540
  467.3 296.3 %reduce-scatter.5.cloned.1.call-start = ((), (), s32[]{:S(2)}) async-start(), calls=%async_computation.3 | async-start | bytes 294912
Sparse Core Ops, SparseCore 0:
  82.4 286.1 all-reduce.5
  371.1 55.5 all-gather.2
  467.4 254.0 all-reduce.3
  724.4 39.1 reduce-scatter.4
where the time goes:
time: 771 us; the launch traced here: 770 us
  waiting for transfers between devices  533 us (69%)
  blocking collectives  107 us (14%)
  matrix products  57.4 us (7%)
  local copies, waits for them, and re-layouts  55.4 us (7%)
  between operations  14.5 us (2%)
    unnamed x6, waiting for transfers between devices  247 us
    psum x1, waiting for transfers between devices, body(): grad_weight, grad_bias = lax.psum((weight_term, bias_term), ('row', 'col'))  230 us
    psum x1, blocking collectives, body(): grad_weight, grad_bias = lax.psum((weight_term, bias_term), ('row', 'col'))  77.5 us
    all_gather x1, waiting for transfers between devices, body(): right_all = lax.all_gather(right, 'row', axis=0, tiled=True)  55.6 us
    all_gather x1, blocking collectives, body(): left_all = lax.all_gather(left, 'col', axis=0, tiled=True)  29.5 us
    dot_general x1, matrix products, body(): jnp.einsum('icje,cez->ijz', outer_split, weight_cube, precision=highest)  17.6 us
  transfers between devices with their start and end apart: 4, of which 4 were waited for; matrix products, arithmetic and copies ran while one was open for 4% of the time, Pallas kernels for 0%

commit v1 on v0

--- a/solution.py
+++ b/solution.py
@@ -9,6 +9,10 @@
 
 
 def body(left, right, w_out, b_out, pair_grad):
+
+    def start_cells(matrix):
+        return lax.psum(lax.psum(matrix, axis_name="row"), axis_name="col")
+
     highest = lax.Precision.HIGHEST
     tile_rows = left.shape[1] // C
     tile_cols = right.shape[1] // C
@@ -52,7 +56,7 @@
         C * C, Z
     )
     bias_term = jnp.sum(pair_grad, axis=(0, 1))
-    grad_weight, grad_bias = lax.psum((weight_term, bias_term), ("row", "col"))
+    grad_weight, grad_bias = start_cells((weight_term, bias_term))
     return (pair_out, grad_left, grad_right, grad_weight / residues, grad_bias / residues)
 
 

time: 771 us -> 551 us (0.71)
  waiting for transfers between devices: 533 us -> 305 us
    psum x1, waiting for transfers between devices: 230 us -> 62 us  [start_cells(): return lax.psum(lax.psum(matrix, axis_name='row'), axis_name='col')]
    all_gather x1, waiting for transfers between devices: 55.6 us -> 0.01 us  [body(): right_all = lax.all_gather(right, 'row', axis=0, tiled=True)]
    psum x1 -> x2, blocking collectives: 77.5 us -> 84.7 us  [start_cells(): return lax.psum(lax.psum(matrix, axis_name='row'), axis_name='col')]
  transfers between devices with their start and end apart: 4 -> 4, of which waited for: 4 -> 3; matrix products, arithmetic and copies ran while one was open for 4% -> 13% of each run, Pallas kernels for 0% -> 0%
where the time goes in v1:
time: 551 us; the launch traced here: 549 us
  waiting for transfers between devices  305 us (55%)
  blocking collectives  114 us (21%)
  matrix products  57.8 us (10%)
  local copies, waits for them, and re-layouts  54.6 us (10%)
  between operations  14.5 us (3%)
    unnamed x6, waiting for transfers between devices  243 us
    psum x2, blocking collectives, start_cells(): return lax.psum(lax.psum(matrix, axis_name='row'), axis_name='col')  84.7 us
    psum x1, waiting for transfers between devices, start_cells(): return lax.psum(lax.psum(matrix, axis_name='row'), axis_name='col')  62 us
    all_gather x1, blocking collectives, body(): left_all = lax.all_gather(left, 'col', axis=0, tiled=True)  29.8 us
    dot_general x1, matrix products, body(): jnp.einsum('icje,cez->ijz', outer_split, weight_cube, precision=highest)  17.7 us
    reshape x1, local copies, waits for them, and re-layouts, body(): grad_outer = grad_outer.reshape(tile_rows * C, tile_cols * C)  13.4 us
    dot_general x1, local copies, waits for them, and re-layouts, body(): jnp.einsum('icje,ijz->cez', outer_split, pair_grad, precision=highest)  12.8 us
    transpose x1, local copies, waits for them, and re-layouts, body(): jnp.einsum('ijz,cez->icje', pair_grad, weight_cube, precision=highest)  12.4 us
  transfers between devices with their start and end apart: 4, of which 3 were waited for; matrix products, arithmetic and copies ran while one was open for 13% of the time, Pallas kernels for 0%

profile of v1, /device:TPU:8, one launch (start us, length us, event | category | flops | bytes accessed | tf_op | source)
XLA Modules:
  0.0 549.5 jit_solution(5579469853500991909)
XLA Ops:
  7.2 0.7 all-gather.3.cloned.1.call-update
  8.2 9.8 %convolution_bitcast_fusion = f32[16,32,64,32]{2,3,0,1:T(8,128)} fusion(f32[32,32,128,1]{2,1,3,0:T(8,128)S(1)} %bitcast.43, f32[16,64,128]{2,1,0:T(8,128)} %param.9), kind=kOutput, calls=%fused_computation.1 | convolution fusion | flops 1610612736 | bytes 5242880 | tf_op jit(solution)/shard_map/ijz,cez->icje/dot_general | solution.py:37
  18.0 12.4 %copy.21 = f32[16,32,64,32]{3,2,1,0:T(8,128)} copy(f32[16,32,64,32]{2,3,0,1:T(8,128)} %convolution_bitcast_fusion) | data formatting | bytes 8388608 | tf_op jit(solution)/shard_map/ijz,cez->icje/transpose | solution.py:37
  30.4 13.4 %reshape.24 = f32[512,2048]{1,0:T(8,128)} reshape(f32[16,32,64,32]{3,2,1,0:T(8,128)} %copy.21) | data formatting | bytes 8388608 | tf_op jit(solution)/shard_map/reshape | solution.py:38
  43.8 29.8 %all_gather.6 = f32[128,512]{1,0:T(8,128)S(1)} all-gather(f32[16,512]{1,0:T(8,128)S(1)} %copy-done.3), channel_id=1, replica_groups=mesh['row'=32,'col'=8] {'col'}, dimensions={0}, use_global_device_ids=true | all-gather | bytes 294912 | tf_op jit(solution)/shard_map/all_gather | solution.py:23
  73.6 9.9 %fusion = f32[128,2048]{0,1:T(8,128)} fusion(f32[512,2048]{1,0:T(8,128)} %reshape.24, f32[128,512]{1,0:T(8,128)S(1)} %all_gather.6), kind=kOutput, calls=%fused_computation.3 | convolution fusion | flops 1610874880 | bytes 5505024 | tf_op jit(solution)/shard_map/dot_general | solution.py:53
  83.5 1.6 reshape.26
  85.1 5.4 convolution_multiply_fusion
  90.4 11.4 %reshape.22 = f32[16,32,64,32]{3,2,1,0:T(8,128)} reshape(f32[512,2048]{1,0:T(8,128)} %convolution_multiply_fusion) | data formatting | bytes 8388608 | tf_op jit(solution)/shard_map/reshape | solution.py:35
  101.9 12.8 %copy.33 = f32[32,32,16,64]{3,1,0,2:T(8,128)} copy(f32[32,32,16,64]{1,3,0,2:T(8,128)} %bitcast.44) | data formatting | bytes 8388608 | tf_op jit(solution)/shard_map/icje,ijz->cez/dot_general | solution.py:55
  114.7 9.9 %convolution_bitcast_fusion.2 = f32[1024,128]{1,0:T(8,128)} fusion(f32[1024,16,64]{2,0,1:T(8,128)} %bitcast.45, f32[16,64,128]{2,1,0:T(8,128)S(1)} %copy-done.1), kind=kOutput, calls=%fused_computation.5 | convolution fusion | flops 1610612736 | bytes 5242880 | tf_op jit(solution)/shard_map/icje,ijz->cez/dot_general | solution.py:55
  124.8 0.6 dynamic-slice
  126.0 65.8 %psum.30 = f32[128]{0:T(128)S(1)} all-reduce(f32[128]{0:T(128)S(1)} %reduce_sum.9), channel_id=1, replica_groups=mesh['row'=32,'col'=8] {'row'}, use_global_device_ids=true, to_apply=%region_5.0 | all-reduce | flops 128 | bytes 1024 | tf_op jit(solution)/shard_map/psum | solution.py:14
  191.8 18.9 %psum.31 = f32[128]{0:T(128)S(1)} all-reduce(f32[128]{0:T(128)S(1)} %psum.30), channel_id=1, replica_groups=mesh['row'=32,'col'=8] {'col'}, use_global_device_ids=true, to_apply=%region_6.0 | all-reduce | flops 128 | bytes 1024 | tf_op jit(solution)/shard_map/psum | solution.py:14
  210.7 201.9 %all-reduce.7.cloned.1.call-done = (f32[128,2048]{0,1:T(8,128)}, f32[1024,128]{1,0:T(8,128)}) async-done(((f32[128,2048]{0,1:T(8,128)}, f32[1024,128]{1,0:T(8,128)}), (f32[128,2048]{0,1:T(8,128)}, f32[1024,128]{1,0:T(8,128)})) %all-reduce.7.cloned.1.call-update) | async-done | bytes 1572880
  412.7 0.5 broadcast_multiply_fusion.1
  413.2 5.2 fusion.2
  418.4 0.8 copy.29
  419.3 17.7 %fusion.1 = f32[16,64,128]{2,1,0:T(8,128)} fusion(f32[16,32,64,32]{3,2,1,0:T(8,128)} %reshape.22, f32[32,32,128,1]{2,1,0,3:T(8,128)S(1)} %bitcast.42, f32[128]{0:T(128)S(1)} %copy-done.4), kind=kOutput, calls=%fused_computation.6 | convolution fusion | flops 1610743808 | bytes 5243392 | tf_op jit(solution)/shard_map/icje,cez->ijz/dot_general | solution.py:36
  437.0 0.3 constant_dynamic-slice_fusion
  437.3 0.9 copy.25
  438.3 62.0 %all-reduce.5.cloned.1.call-done = f32[1024,128]{1,0:T(8,128)} async-done(((f32[1024,128]{1,0:T(8,128)}), f32[1024,128]{1,0:T(8,128)}) %all-reduce.5.cloned.1.call-update) | async-done | bytes 524304 | tf_op jit(solution)/shard_map/psum | solution.py:14
  500.2 1.9 broadcast_multiply_fusion
  502.1 40.9 %reduce-scatter.5.cloned.1.call-done = f32[16,512]{1,0:T(8,128)} async-done(((f32[128,512]{1,0:T(8,128)}), f32[16,512]{1,0:T(8,128)}) %reduce-scatter.5.cloned.1.call-update) | async-done | bytes 32784
  (21 shorter events, 0.6 us)
Async XLA Ops:
  7.2 1.0 copy-start
  7.2 76.3 %all-gather.3.cloned.1.call-start = ((), (), s32[]{:S(2)}) async-start(), calls=%async_computation.2 | async-start | bytes 1081344 | tf_op jit(solution)/shard_map/all_gather | solution.py:24
  7.9 404.7 %all-reduce.7.cloned.1.call-start = ((), (), s32[]{:S(2)}) async-start(), calls=%async_computation.4 | async-start | bytes 3145728
  30.4 13.4 %copy-start.3 = (f32[16,512]{1,0:T(8,128)S(1)}, f32[16,512]{1,0:T(8,128)}, u32[]{:S(2)}) copy-start(f32[16,512]{1,0:T(8,128)} %param.5) | copy-start | bytes 98308
  101.9 12.8 %copy-start.1 = (f32[16,64,128]{2,1,0:T(8,128)S(1)}, f32[16,64,128]{2,1,0:T(8,128)}, u32[]{:S(2)}) copy-start(f32[16,64,128]{2,1,0:T(8,128)} %param.9) | copy-start | bytes 1572868
  114.7 10.1 %copy-start.5 = (u32[256]{0:T(256)S(1)}, u32[256]{0:T(256)}, u32[]{:S(2)}) copy-start(u32[256]{0:T(256)} %constant.18) | copy-start | bytes 3076
  114.7 304.6 %copy-start.4 = (f32[128]{0:T(128)S(1)}, f32[128]{0:T(128)}, u32[]{:S(2)}) copy-start(f32[128]{0:T(128)} %param.8) | copy-start | bytes 1540
  124.6 375.6 %all-reduce.5.cloned.1.call-start = ((), (), s32[]{:S(2)}) async-start(), calls=%async_computation.1 | async-start | bytes 1048576 | tf_op jit(solution)/shard_map/psum | solution.py:14
  412.7 130.3 %reduce-scatter.5.cloned.1.call-start = ((), (), s32[]{:S(2)}) async-start(), calls=%async_computation.3 | async-start | bytes 294912
  419.3 17.7 %copy-start.2 = (f32[128,2048]{0,1:T(8,128)S(1)}, f32[128,2048]{0,1:T(8,128)}, u32[]{:S(2)}) copy-start(f32[128,2048]{0,1:T(8,128)} %get-tuple-element.20) | copy-start | bytes 3145732
Sparse Core Ops, SparseCore 0:
  10.5 53.8 all-gather.2
  124.7 287.8 all-reduce.6
  415.3 84.9 all-reduce.4
  503.1 39.7 reduce-scatter.4
